TPU v7x, 128 devices: a whole 4x4x4 slice. The times are simulated.
128 devices in a mesh: seq: 32 (over y, z, core), chan: 4 (over x).
Axes of the slice: x: 4, y: 4, z: 4, core: 2. Of those that a mesh axis runs over, the one named last changes fastest.
Arguments:
- tokens: bfloat16 [16384, 4096], P('seq', 'chan'), may hold values from -6 to 6
- in_weight: bfloat16 [4096, 3, 2048], P(None, None, 'chan'), may hold values from -0.09375 to 0.09375
- short_weight: float32 [3, 3, 2048], P(None, None, 'chan'), may hold values from -3 to 3
- filter_taps: float32 [16384, 2048], P('seq', 'chan'), may hold values from -1.1 to 1.1
- skip_gain: float32 [2048], P('chan'), may hold values from -3 to 3
Outputs:
- hyena_out: bfloat16 [16384, 2048], P('seq', 'chan')
All inputs are finite; a program needn't handle non-finite values.
Results may differ from a plain program's by a relative error of at most 0.012.
Values may be sent and summed in bfloat16 or wider, within the bound.
A program may use at most 128 MiB of HBM per device.

v0:
```python
import math

import jax
import jax.numpy as jnp
from jax import lax
from jax.sharding import PartitionSpec as P

precise = lax.Precision.HIGHEST


def swapped(array, axis, apart):
    return lax.ppermute(array, axis, [(i, i ^ 1 << apart) for i in range(lax.axis_size(axis))])


def passed_along(array, axis, by):
    peers = lax.axis_size(axis)
    pairs = [(i, i + by) for i in range(peers) if 0 <= i + by < peers]
    return lax.ppermute(array, axis, pairs)


def angles_of(counts, period):
    return -2.0 * math.pi / period * counts.astype(jnp.float32)


def reverse_bits(device, seq_count):
    sections = seq_count.bit_length() - 1
    reversed_index = jnp.zeros((), jnp.int32)
    for bit_index in range(sections):
        reversed_index = reversed_index + device // 2**bit_index % 2 * 2 ** (
            sections - 1 - bit_index
        )
    return reversed_index


def spread_halves(values, position, double_len):
    angle_vals = angles_of(position, double_len)[:, None]
    real_part = jnp.stack([values, values * jnp.cos(angle_vals)])
    imag_part = jnp.stack([jnp.zeros_like(values), values * jnp.sin(angle_vals)])
    return (real_part, imag_part)


def local_table(seg_rows, start_freq, stride, length):
    row_ids = lax.broadcasted_iota(jnp.int32, (seg_rows, seg_rows), 0)
    col_ids = lax.broadcasted_iota(jnp.int32, (seg_rows, seg_rows), 1)
    counts = col_ids * (start_freq + stride * row_ids) % length
    angle_vals = angles_of(counts, length)
    return (jnp.cos(angle_vals), jnp.sin(angle_vals))


def local_forward(cos_tab, sin_tab, real_part, imag_part):
    out_real = jnp.einsum("rj,ejc->erc", cos_tab, real_part, precision=precise) - jnp.einsum(
        "rj,ejc->erc", sin_tab, imag_part, precision=precise
    )
    out_imag = jnp.einsum("rj,ejc->erc", cos_tab, imag_part, precision=precise) + jnp.einsum(
        "rj,ejc->erc", sin_tab, real_part, precision=precise
    )
    return (out_real, out_imag)


def local_inverse(cos_tab, sin_tab, real_part, imag_part):
    out_real = jnp.einsum("rj,erc->ejc", cos_tab, real_part, precision=precise) + jnp.einsum(
        "rj,erc->ejc", sin_tab, imag_part, precision=precise
    )
    out_imag = jnp.einsum("rj,erc->ejc", cos_tab, imag_part, precision=precise) - jnp.einsum(
        "rj,erc->ejc", sin_tab, real_part, precision=precise
    )
    return (out_real, out_imag)


def pair_forward(real_part, imag_part, device, seq_count):
    half_span = seq_count // 2
    while half_span >= 1:
        bit_index = half_span.bit_length() - 1
        other_real, other_imag = swapped((real_part, imag_part), "seq", bit_index)
        is_upper = device // half_span % 2 == 1
        angle_vals = angles_of(device % half_span * (seq_count // (2 * half_span)), seq_count)
        cosine = jnp.cos(angle_vals)
        sine_vals = jnp.sin(angle_vals)
        diff_real = other_real - real_part
        diff_imag = other_imag - imag_part
        rot_real = diff_real * cosine - diff_imag * sine_vals
        rot_imag = diff_real * sine_vals + diff_imag * cosine
        real_part = jnp.where(is_upper, rot_real, real_part + other_real)
        imag_part = jnp.where(is_upper, rot_imag, imag_part + other_imag)
        half_span = half_span // 2
    return (real_part, imag_part)


def pair_inverse(real_part, imag_part, device, seq_count):
    half_span = 1
    while half_span < seq_count:
        bit_index = half_span.bit_length() - 1
        other_real, other_imag = swapped((real_part, imag_part), "seq", bit_index)
        is_upper = device // half_span % 2 == 1
        angle_vals = angles_of(device % half_span * (seq_count // (2 * half_span)), seq_count)
        cosine = jnp.cos(angle_vals)
        sine_vals = jnp.sin(angle_vals)
        other_rot_real = other_real * cosine + other_imag * sine_vals
        other_rot_imag = other_imag * cosine - other_real * sine_vals
        mine_rot_real = real_part * cosine + imag_part * sine_vals
        mine_rot_imag = imag_part * cosine - real_part * sine_vals
        new_real = jnp.where(is_upper, other_real - mine_rot_real, real_part + other_rot_real)
        new_imag = jnp.where(is_upper, other_imag - mine_rot_imag, imag_part + other_rot_imag)
        real_part = new_real
        imag_part = new_imag
        half_span = half_span * 2
    return (real_part, imag_part)


def local(tokens, in_weight, short_weight, filter_taps, skip_gain):
    seg_rows = tokens.shape[0]
    seq_count = lax.axis_size("seq")
    device = lax.axis_index("seq")
    length = seg_rows * seq_count
    double_len = 2 * length
    position = device * seg_rows + lax.iota(jnp.int32, seg_rows)
    projected = jnp.einsum(
        "td,dgc->tgc",
        lax.all_gather(tokens, "chan", axis=1, tiled=True),
        in_weight,
        preferred_element_type=jnp.float32,
    ).astype(jnp.bfloat16)
    previous = passed_along(projected[seg_rows - 2 :], "seq", 1)
    extended = jnp.concatenate([previous, projected], axis=0).astype(jnp.float32)
    shorted = (
        short_weight[0] * extended[2:]
        + short_weight[1] * extended[1:-1]
        + short_weight[2] * extended[:-2]
    ).astype(jnp.bfloat16)
    short_f32 = shorted.astype(jnp.float32)
    mixed_in = short_f32[:, 1] * short_f32[:, 2]
    start_freq = reverse_bits(device, seq_count)
    cos_tab, sin_tab = local_table(seg_rows, start_freq, seq_count, length)

    def forward_spectrum(values):
        real_part, imag_part = spread_halves(values, position, double_len)
        real_part, imag_part = pair_forward(real_part, imag_part, device, seq_count)
        return local_forward(cos_tab, sin_tab, real_part, imag_part)

    filter_real, filter_imag = forward_spectrum(filter_taps)
    data_real, data_imag = forward_spectrum(mixed_in)
    prod_real = data_real * filter_real - data_imag * filter_imag
    prod_imag = data_real * filter_imag + data_imag * filter_real
    back_real, back_imag = local_inverse(cos_tab, sin_tab, prod_real, prod_imag)
    time_real, time_imag = pair_inverse(back_real, back_imag, device, seq_count)
    angle_vals = angles_of(position, double_len)[:, None]
    conv_vals = (
        time_real[0] + jnp.cos(angle_vals) * time_real[1] + jnp.sin(angle_vals) * time_imag[1]
    ) / double_len
    hyena_out = ((conv_vals + skip_gain * mixed_in) * short_f32[:, 0]).astype(jnp.bfloat16)
    return hyena_out


def solution(mesh):
    return jax.shard_map(
        local,
        mesh=mesh,
        in_specs=(
            P("seq", "chan"),
            P(None, None, "chan"),
            P(None, None, "chan"),
            P("seq", "chan"),
            P("chan"),
        ),
        out_specs=P("seq", "chan"),
        check_vma=False,
    )
```

profile of v0, /device:TPU:1, one launch (start us, length us, event | category | flops | bytes accessed | tf_op | source)
XLA Modules:
  0.0 1184.4 jit_solution(2023567520953352680)
XLA Ops:
  16.2 44.1 %all-gather.2.cloned.1.call-done = bf16[512,4096]{1,0:T(8,128)(2,1)} async-done(((bf16[512,1024]{1,0:T(8,128)(2,1)}), bf16[512,4096]{1,0:T(8,128)(2,1)}) %all-gather.2.cloned.1.call-update) | async-done | bytes 4194320 | tf_op jit(solution)/shard_map/all_gather | solution.py:119
  60.2 10.9 fusion.13
  84.2 20.4 %collective-permute-done.12 = f32[2,512,512]{2,1,0:T(8,128)} collective-permute-done((f32[2,512,512]{2,1,0:T(8,128)}, f32[2,512,512]{2,1,0:T(8,128)}, u32[]{:S(2)}, u32[]{:S(2)}) %collective-permute-start.12) | collective-permute-done | bytes 2097184 | tf_op jit(solution)/shard_map/ppermute | solution.py:12
  112.3 37.3 %collective-permute-done.2 = f32[2,512,512]{2,1,0:T(8,128)} collective-permute-done((f32[2,512,512]{2,1,0:T(8,128)}, f32[2,512,512]{2,1,0:T(8,128)}, u32[]{:S(2)}, u32[]{:S(2)}) %collective-permute-start.2) | collective-permute-done | bytes 2097184 | tf_op jit(solution)/shard_map/ppermute | solution.py:12
  149.5 44.9 %collective-permute-done.1 = f32[2,512,512]{2,1,0:T(8,128)} collective-permute-done((f32[2,512,512]{2,1,0:T(8,128)}, f32[2,512,512]{2,1,0:T(8,128)}, u32[]{:S(2)}, u32[]{:S(2)}) %collective-permute-start.1) | collective-permute-done | bytes 2097184 | tf_op jit(solution)/shard_map/ppermute | solution.py:12
  201.2 37.5 %collective-permute-done.13 = f32[2,512,512]{2,1,0:T(8,128)} collective-permute-done((f32[2,512,512]{2,1,0:T(8,128)}, f32[2,512,512]{2,1,0:T(8,128)}, u32[]{:S(2)}, u32[]{:S(2)}) %collective-permute-start.13) | collective-permute-done | bytes 2097184 | tf_op jit(solution)/shard_map/ppermute | solution.py:12
  238.6 44.9 %collective-permute-done.14 = f32[2,512,512]{2,1,0:T(8,128)} collective-permute-done((f32[2,512,512]{2,1,0:T(8,128)}, f32[2,512,512]{2,1,0:T(8,128)}, u32[]{:S(2)}, u32[]{:S(2)}) %collective-permute-start.14) | collective-permute-done | bytes 2097184 | tf_op jit(solution)/shard_map/ppermute | solution.py:12
  295.0 33.5 %collective-permute-done.4 = f32[2,512,512]{2,1,0:T(8,128)} collective-permute-done((f32[2,512,512]{2,1,0:T(8,128)}, f32[2,512,512]{2,1,0:T(8,128)}, u32[]{:S(2)}, u32[]{:S(2)}) %collective-permute-start.4) | collective-permute-done | bytes 2097184 | tf_op jit(solution)/shard_map/ppermute | solution.py:12
  328.5 44.9 %collective-permute-done.3 = f32[2,512,512]{2,1,0:T(8,128)} collective-permute-done((f32[2,512,512]{2,1,0:T(8,128)}, f32[2,512,512]{2,1,0:T(8,128)}, u32[]{:S(2)}, u32[]{:S(2)}) %collective-permute-start.3) | collective-permute-done | bytes 2097184 | tf_op jit(solution)/shard_map/ppermute | solution.py:12
  396.5 33.1 %collective-permute-done.6 = f32[2,512,512]{2,1,0:T(8,128)} collective-permute-done((f32[2,512,512]{2,1,0:T(8,128)}, f32[2,512,512]{2,1,0:T(8,128)}, u32[]{:S(2)}, u32[]{:S(2)}) %collective-permute-start.6) | collective-permute-done | bytes 2097184 | tf_op jit(solution)/shard_map/ppermute | solution.py:12
  429.6 44.9 %collective-permute-done.5 = f32[2,512,512]{2,1,0:T(8,128)} collective-permute-done((f32[2,512,512]{2,1,0:T(8,128)}, f32[2,512,512]{2,1,0:T(8,128)}, u32[]{:S(2)}, u32[]{:S(2)}) %collective-permute-start.5) | collective-permute-done | bytes 2097184 | tf_op jit(solution)/shard_map/ppermute | solution.py:12
  486.6 38.4 %collective-permute-done.17 = f32[2,512,512]{2,1,0:T(8,128)} collective-permute-done((f32[2,512,512]{2,1,0:T(8,128)}, f32[2,512,512]{2,1,0:T(8,128)}, u32[]{:S(2)}, u32[]{:S(2)}) %collective-permute-start.17) | collective-permute-done | bytes 2097184 | tf_op jit(solution)/shard_map/ppermute | solution.py:12
  525.0 44.9 %collective-permute-done.18 = f32[2,512,512]{2,1,0:T(8,128)} collective-permute-done((f32[2,512,512]{2,1,0:T(8,128)}, f32[2,512,512]{2,1,0:T(8,128)}, u32[]{:S(2)}, u32[]{:S(2)}) %collective-permute-start.18) | collective-permute-done | bytes 2097184 | tf_op jit(solution)/shard_map/ppermute | solution.py:12
  577.1 37.8 %collective-permute-done.8 = f32[2,512,512]{2,1,0:T(8,128)} collective-permute-done((f32[2,512,512]{2,1,0:T(8,128)}, f32[2,512,512]{2,1,0:T(8,128)}, u32[]{:S(2)}, u32[]{:S(2)}) %collective-permute-start.8) | collective-permute-done | bytes 2097184 | tf_op jit(solution)/shard_map/ppermute | solution.py:12
  614.9 44.9 %collective-permute-done.7 = f32[2,512,512]{2,1,0:T(8,128)} collective-permute-done((f32[2,512,512]{2,1,0:T(8,128)}, f32[2,512,512]{2,1,0:T(8,128)}, u32[]{:S(2)}, u32[]{:S(2)}) %collective-permute-start.7) | collective-permute-done | bytes 2097184 | tf_op jit(solution)/shard_map/ppermute | solution.py:12
  671.3 11.4 fusion.40
  682.8 11.2 fusion.44
  694.0 11.8 convolution_add_fusion
  705.8 11.6 convolution_subtract_fusion
  722.0 11.2 fusion.46
  733.2 11.6 fusion.42
  744.9 11.4 convolution_subtract_fusion.1
  756.3 12.1 %multiply_subtract_fusion = (f32[2,512,512]{2,1,0:T(8,128)S(1)}, f32[2,512,512]{2,1,0:T(8,128)S(1)}) fusion(f32[2,512,512]{2,1,0:T(8,128)S(1)} %convolution_add_fusion, f32[2,512,512]{2,1,0:T(8,128)S(1)} %convolution_subtract_fusion.1, f32[2,512,512]{2,1,0:T(8,128)S(1)} %convolution_subtract_fusion, f32[2,512,512]{2,1,0:T(8,128)S(1)} %fusion.42, ...), kind=kOutput, calls=%fused_computation.30 | convolution fusion | flops 3228565504 | bytes 14682112 | tf_op jit(solution)/shard_map/rj,ejc->erc/dot_general | solution.py:54
  775.9 7.9 fusion.7
  806.4 45.6 %collective-permute-done.23 = f32[2,512,512]{2,1,0:T(8,128)S(1)} collective-permute-done((f32[2,512,512]{2,1,0:T(8,128)S(1)}, f32[2,512,512]{2,1,0:T(8,128)S(1)}, u32[]{:S(2)}, u32[]{:S(2)}) %collective-permute-start.23) | collective-permute-done | bytes 2097184 | tf_op jit(solution)/shard_map/ppermute | solution.py:12
  852.0 44.9 %collective-permute-done.24 = f32[2,512,512]{2,1,0:T(8,128)S(1)} collective-permute-done((f32[2,512,512]{2,1,0:T(8,128)S(1)}, f32[2,512,512]{2,1,0:T(8,128)S(1)}, u32[]{:S(2)}, u32[]{:S(2)}) %collective-permute-start.24) | collective-permute-done | bytes 2097184 | tf_op jit(solution)/shard_map/ppermute | solution.py:12
  901.4 44.5 %collective-permute-done.25 = f32[2,512,512]{2,1,0:T(8,128)S(1)} collective-permute-done((f32[2,512,512]{2,1,0:T(8,128)S(1)}, f32[2,512,512]{2,1,0:T(8,128)S(1)}, u32[]{:S(2)}, u32[]{:S(2)}) %collective-permute-start.25) | collective-permute-done | bytes 2097184 | tf_op jit(solution)/shard_map/ppermute | solution.py:12
  945.9 44.9 %collective-permute-done.26 = f32[2,512,512]{2,1,0:T(8,128)S(1)} collective-permute-done((f32[2,512,512]{2,1,0:T(8,128)S(1)}, f32[2,512,512]{2,1,0:T(8,128)S(1)}, u32[]{:S(2)}, u32[]{:S(2)}) %collective-permute-start.26) | collective-permute-done | bytes 2097184 | tf_op jit(solution)/shard_map/ppermute | solution.py:12
  993.6 43.9 %collective-permute-done.27 = f32[2,512,512]{2,1,0:T(8,128)S(1)} collective-permute-done((f32[2,512,512]{2,1,0:T(8,128)S(1)}, f32[2,512,512]{2,1,0:T(8,128)S(1)}, u32[]{:S(2)}, u32[]{:S(2)}) %collective-permute-start.27) | collective-permute-done | bytes 2097184 | tf_op jit(solution)/shard_map/ppermute | solution.py:12
  1037.5 44.9 %collective-permute-done.28 = f32[2,512,512]{2,1,0:T(8,128)S(1)} collective-permute-done((f32[2,512,512]{2,1,0:T(8,128)S(1)}, f32[2,512,512]{2,1,0:T(8,128)S(1)}, u32[]{:S(2)}, u32[]{:S(2)}) %collective-permute-start.28) | collective-permute-done | bytes 2097184 | tf_op jit(solution)/shard_map/ppermute | solution.py:12
  1086.7 43.0 %collective-permute-done.29 = f32[2,512,512]{2,1,0:T(8,128)S(1)} collective-permute-done((f32[2,512,512]{2,1,0:T(8,128)S(1)}, f32[2,512,512]{2,1,0:T(8,128)S(1)}, u32[]{:S(2)}, u32[]{:S(2)}) %collective-permute-start.29) | collective-permute-done | bytes 2097184 | tf_op jit(solution)/shard_map/ppermute | solution.py:12
  1129.7 44.9 %collective-permute-done.30 = f32[2,512,512]{2,1,0:T(8,128)S(1)} collective-permute-done((f32[2,512,512]{2,1,0:T(8,128)S(1)}, f32[2,512,512]{2,1,0:T(8,128)S(1)}, u32[]{:S(2)}, u32[]{:S(2)}) %collective-permute-start.30) | collective-permute-done | bytes 2097184 | tf_op jit(solution)/shard_map/ppermute | solution.py:12
  (98 shorter events, 150.0 us)
Async XLA Ops:
  6.5 53.7 %all-gather.2.cloned.1.call-start = ((), (), s32[]{:S(2)}) async-start(), calls=%async_computation | async-start | bytes 5242880 | tf_op jit(solution)/shard_map/all_gather | solution.py:119
  10.5 73.7 %collective-permute-start.11 = (f32[2,512,512]{2,1,0:T(8,128)}, f32[2,512,512]{2,1,0:T(8,128)}, u32[]{:S(2)}, u32[]{:S(2)}) collective-permute-start(f32[2,512,512]{2,1,0:T(8,128)} %pad_maximum_fusion.1), channel_id=1, source_target_pairs={{0,64},{4,68},{8,72},{12,76},{16,80},{20,84},{24,88},{28,92},{32,9... | collective-permute-start | bytes 6291464 | tf_op jit(solution)/shard_map/ppermute | solution.py:12
  15.9 88.7 %collective-permute-start.12 = (f32[2,512,512]{2,1,0:T(8,128)}, f32[2,512,512]{2,1,0:T(8,128)}, u32[]{:S(2)}, u32[]{:S(2)}) collective-permute-start(f32[2,512,512]{2,1,0:T(8,128)} %stack.30), channel_id=1, source_target_pairs={{0,64},{4,68},{8,72},{12,76},{16,80},{20,84},{24,88},{28,92},{32,9... | collective-permute-start | bytes 6291464 | tf_op jit(solution)/shard_map/ppermute | solution.py:12
  71.1 4.7 collective-permute-start
  79.2 70.3 %collective-permute-start.2 = (f32[2,512,512]{2,1,0:T(8,128)}, f32[2,512,512]{2,1,0:T(8,128)}, u32[]{:S(2)}, u32[]{:S(2)}) collective-permute-start(f32[2,512,512]{2,1,0:T(8,128)} %stack.25), channel_id=1, source_target_pairs={{0,64},{4,68},{8,72},{12,76},{16,80},{20,84},{24,88},{28,92},{32,9... | collective-permute-start | bytes 6291464 | tf_op jit(solution)/shard_map/ppermute | solution.py:12
  83.7 110.8 %collective-permute-start.1 = (f32[2,512,512]{2,1,0:T(8,128)}, f32[2,512,512]{2,1,0:T(8,128)}, u32[]{:S(2)}, u32[]{:S(2)}) collective-permute-start(f32[2,512,512]{2,1,0:T(8,128)} %pad_maximum_fusion), channel_id=1, source_target_pairs={{0,64},{4,68},{8,72},{12,76},{16,80},{20,84},{24,88},{28,92},{32,9... | collective-permute-start | bytes 6291464 | tf_op jit(solution)/shard_map/ppermute | solution.py:12
  110.8 127.8 %collective-permute-start.13 = (f32[2,512,512]{2,1,0:T(8,128)}, f32[2,512,512]{2,1,0:T(8,128)}, u32[]{:S(2)}, u32[]{:S(2)}) collective-permute-start(f32[2,512,512]{2,1,0:T(8,128)} %get-tuple-element.33), channel_id=1, source_target_pairs={{0,32},{4,36},{8,40},{12,44},{16,48},{20,52},{24,56},{28,60},{32,0... | collective-permute-start | bytes 6291464 | tf_op jit(solution)/shard_map/ppermute | solution.py:12
  112.1 171.5 %collective-permute-start.14 = (f32[2,512,512]{2,1,0:T(8,128)}, f32[2,512,512]{2,1,0:T(8,128)}, u32[]{:S(2)}, u32[]{:S(2)}) collective-permute-start(f32[2,512,512]{2,1,0:T(8,128)} %get-tuple-element.34), channel_id=1, source_target_pairs={{0,32},{4,36},{8,40},{12,44},{16,48},{20,52},{24,56},{28,60},{32,0... | collective-permute-start | bytes 6291464 | tf_op jit(solution)/shard_map/ppermute | solution.py:12
  199.5 129.0 %collective-permute-start.4 = (f32[2,512,512]{2,1,0:T(8,128)}, f32[2,512,512]{2,1,0:T(8,128)}, u32[]{:S(2)}, u32[]{:S(2)}) collective-permute-start(f32[2,512,512]{2,1,0:T(8,128)} %get-tuple-element.35), channel_id=1, source_target_pairs={{0,32},{4,36},{8,40},{12,44},{16,48},{20,52},{24,56},{28,60},{32,0... | collective-permute-start | bytes 6291464 | tf_op jit(solution)/shard_map/ppermute | solution.py:12
  199.5 173.9 %collective-permute-start.3 = (f32[2,512,512]{2,1,0:T(8,128)}, f32[2,512,512]{2,1,0:T(8,128)}, u32[]{:S(2)}, u32[]{:S(2)}) collective-permute-start(f32[2,512,512]{2,1,0:T(8,128)} %get-tuple-element.36), channel_id=1, source_target_pairs={{0,32},{4,36},{8,40},{12,44},{16,48},{20,52},{24,56},{28,60},{32,0... | collective-permute-start | bytes 6291464 | tf_op jit(solution)/shard_map/ppermute | solution.py:12
  290.1 94.9 %collective-permute-start.15 = (f32[2,512,512]{2,1,0:T(8,128)}, f32[2,512,512]{2,1,0:T(8,128)}, u32[]{:S(2)}, u32[]{:S(2)}) collective-permute-start(f32[2,512,512]{2,1,0:T(8,128)} %get-tuple-element.23), channel_id=1, source_target_pairs={{0,16},{4,20},{8,24},{12,28},{16,0},{20,4},{24,8},{28,12},{32,48},... | collective-permute-start | bytes 6291464 | tf_op jit(solution)/shard_map/ppermute | solution.py:12
  294.9 90.1 %collective-permute-start.16 = (f32[2,512,512]{2,1,0:T(8,128)}, f32[2,512,512]{2,1,0:T(8,128)}, u32[]{:S(2)}, u32[]{:S(2)}) collective-permute-start(f32[2,512,512]{2,1,0:T(8,128)} %get-tuple-element.24), channel_id=1, source_target_pairs={{0,16},{4,20},{8,24},{12,28},{16,0},{20,4},{24,8},{28,12},{32,48},... | collective-permute-start | bytes 6291464 | tf_op jit(solution)/shard_map/ppermute | solution.py:12
  380.1 49.5 %collective-permute-start.6 = (f32[2,512,512]{2,1,0:T(8,128)}, f32[2,512,512]{2,1,0:T(8,128)}, u32[]{:S(2)}, u32[]{:S(2)}) collective-permute-start(f32[2,512,512]{2,1,0:T(8,128)} %get-tuple-element.31), channel_id=1, source_target_pairs={{0,16},{4,20},{8,24},{12,28},{16,0},{20,4},{24,8},{28,12},{32,48},... | collective-permute-start | bytes 6291464 | tf_op jit(solution)/shard_map/ppermute | solution.py:12
  384.8 89.7 %collective-permute-start.5 = (f32[2,512,512]{2,1,0:T(8,128)}, f32[2,512,512]{2,1,0:T(8,128)}, u32[]{:S(2)}, u32[]{:S(2)}) collective-permute-start(f32[2,512,512]{2,1,0:T(8,128)} %get-tuple-element.32), channel_id=1, source_target_pairs={{0,16},{4,20},{8,24},{12,28},{16,0},{20,4},{24,8},{28,12},{32,48},... | collective-permute-start | bytes 6291464 | tf_op jit(solution)/shard_map/ppermute | solution.py:12
  391.6 133.4 %collective-permute-start.17 = (f32[2,512,512]{2,1,0:T(8,128)}, f32[2,512,512]{2,1,0:T(8,128)}, u32[]{:S(2)}, u32[]{:S(2)}) collective-permute-start(f32[2,512,512]{2,1,0:T(8,128)} %get-tuple-element.21), channel_id=1, source_target_pairs={{0,8},{4,12},{8,0},{12,4},{16,24},{20,28},{24,16},{28,20},{32,40},... | collective-permute-start | bytes 6291464 | tf_op jit(solution)/shard_map/ppermute | solution.py:12
  396.5 173.5 %collective-permute-start.18 = (f32[2,512,512]{2,1,0:T(8,128)}, f32[2,512,512]{2,1,0:T(8,128)}, u32[]{:S(2)}, u32[]{:S(2)}) collective-permute-start(f32[2,512,512]{2,1,0:T(8,128)} %get-tuple-element.22), channel_id=1, source_target_pairs={{0,8},{4,12},{8,0},{12,4},{16,24},{20,28},{24,16},{28,20},{32,40},... | collective-permute-start | bytes 6291464 | tf_op jit(solution)/shard_map/ppermute | solution.py:12
  481.1 133.8 %collective-permute-start.8 = (f32[2,512,512]{2,1,0:T(8,128)}, f32[2,512,512]{2,1,0:T(8,128)}, u32[]{:S(2)}, u32[]{:S(2)}) collective-permute-start(f32[2,512,512]{2,1,0:T(8,128)} %get-tuple-element.29), channel_id=1, source_target_pairs={{0,8},{4,12},{8,0},{12,4},{16,24},{20,28},{24,16},{28,20},{32,40},... | collective-permute-start | bytes 6291464 | tf_op jit(solution)/shard_map/ppermute | solution.py:12
  486.4 173.4 %collective-permute-start.7 = (f32[2,512,512]{2,1,0:T(8,128)}, f32[2,512,512]{2,1,0:T(8,128)}, u32[]{:S(2)}, u32[]{:S(2)}) collective-permute-start(f32[2,512,512]{2,1,0:T(8,128)} %get-tuple-element.30), channel_id=1, source_target_pairs={{0,8},{4,12},{8,0},{12,4},{16,24},{20,28},{24,16},{28,20},{32,40},... | collective-permute-start | bytes 6291464 | tf_op jit(solution)/shard_map/ppermute | solution.py:12
  576.5 90.2 %collective-permute-start.19 = (f32[2,512,512]{2,1,0:T(8,128)}, f32[2,512,512]{2,1,0:T(8,128)}, u32[]{:S(2)}, u32[]{:S(2)}) collective-permute-start(f32[2,512,512]{2,1,0:T(8,128)} %get-tuple-element.19), channel_id=1, source_target_pairs={{0,4},{4,0},{8,12},{12,8},{16,20},{20,16},{24,28},{28,24},{32,36},... | collective-permute-start | bytes 6291464 | tf_op jit(solution)/shard_map/ppermute | solution.py:12
  576.9 89.9 %collective-permute-start.20 = (f32[2,512,512]{2,1,0:T(8,128)}, f32[2,512,512]{2,1,0:T(8,128)}, u32[]{:S(2)}, u32[]{:S(2)}) collective-permute-start(f32[2,512,512]{2,1,0:T(8,128)} %get-tuple-element.20), channel_id=1, source_target_pairs={{0,4},{4,0},{8,12},{12,8},{16,20},{20,16},{24,28},{28,24},{32,36},... | collective-permute-start | bytes 6291464 | tf_op jit(solution)/shard_map/ppermute | solution.py:12
  666.3 51.2 %collective-permute-start.10 = (f32[2,512,512]{2,1,0:T(8,128)}, f32[2,512,512]{2,1,0:T(8,128)}, u32[]{:S(2)}, u32[]{:S(2)}) collective-permute-start(f32[2,512,512]{2,1,0:T(8,128)} %get-tuple-element.27), channel_id=1, source_target_pairs={{0,4},{4,0},{8,12},{12,8},{16,20},{20,16},{24,28},{28,24},{32,36},... | collective-permute-start | bytes 6291464 | tf_op jit(solution)/shard_map/ppermute | solution.py:12
  666.7 50.8 %collective-permute-start.9 = (f32[2,512,512]{2,1,0:T(8,128)}, f32[2,512,512]{2,1,0:T(8,128)}, u32[]{:S(2)}, u32[]{:S(2)}) collective-permute-start(f32[2,512,512]{2,1,0:T(8,128)} %get-tuple-element.28), channel_id=1, source_target_pairs={{0,4},{4,0},{8,12},{12,8},{16,20},{20,16},{24,28},{28,24},{32,36},... | collective-permute-start | bytes 6291464 | tf_op jit(solution)/shard_map/ppermute | solution.py:12
  791.4 8.3 collective-permute-start.22
  799.5 4.2 collective-permute-start.21
  804.8 47.1 %collective-permute-start.23 = (f32[2,512,512]{2,1,0:T(8,128)S(1)}, f32[2,512,512]{2,1,0:T(8,128)S(1)}, u32[]{:S(2)}, u32[]{:S(2)}) collective-permute-start(f32[2,512,512]{2,1,0:T(8,128)S(1)} %get-tuple-element.14), channel_id=1, source_target_pairs={{0,8},{4,12},{8,0},{12,4},{16,24},{20,28},{24,16},{28,20},{32,40},... | collective-permute-start | bytes 6291464 | tf_op jit(solution)/shard_map/ppermute | solution.py:12
  804.9 92.0 %collective-permute-start.24 = (f32[2,512,512]{2,1,0:T(8,128)S(1)}, f32[2,512,512]{2,1,0:T(8,128)S(1)}, u32[]{:S(2)}, u32[]{:S(2)}) collective-permute-start(f32[2,512,512]{2,1,0:T(8,128)S(1)} %get-tuple-element.13), channel_id=1, source_target_pairs={{0,8},{4,12},{8,0},{12,4},{16,24},{20,28},{24,16},{28,20},{32,40},... | collective-permute-start | bytes 6291464 | tf_op jit(solution)/shard_map/ppermute | solution.py:12
  898.1 47.8 %collective-permute-start.25 = (f32[2,512,512]{2,1,0:T(8,128)S(1)}, f32[2,512,512]{2,1,0:T(8,128)S(1)}, u32[]{:S(2)}, u32[]{:S(2)}) collective-permute-start(f32[2,512,512]{2,1,0:T(8,128)S(1)} %get-tuple-element.12), channel_id=1, source_target_pairs={{0,16},{4,20},{8,24},{12,28},{16,0},{20,4},{24,8},{28,12},{32,48},... | collective-permute-start | bytes 6291464 | tf_op jit(solution)/shard_map/ppermute | solution.py:12
  898.9 92.0 %collective-permute-start.26 = (f32[2,512,512]{2,1,0:T(8,128)S(1)}, f32[2,512,512]{2,1,0:T(8,128)S(1)}, u32[]{:S(2)}, u32[]{:S(2)}) collective-permute-start(f32[2,512,512]{2,1,0:T(8,128)S(1)} %get-tuple-element.11), channel_id=1, source_target_pairs={{0,16},{4,20},{8,24},{12,28},{16,0},{20,4},{24,8},{28,12},{32,48},... | collective-permute-start | bytes 6291464 | tf_op jit(solution)/shard_map/ppermute | solution.py:12
  992.1 45.4 %collective-permute-start.27 = (f32[2,512,512]{2,1,0:T(8,128)S(1)}, f32[2,512,512]{2,1,0:T(8,128)S(1)}, u32[]{:S(2)}, u32[]{:S(2)}) collective-permute-start(f32[2,512,512]{2,1,0:T(8,128)S(1)} %get-tuple-element.10), channel_id=1, source_target_pairs={{0,32},{4,36},{8,40},{12,44},{16,48},{20,52},{24,56},{28,60},{32,0... | collective-permute-start | bytes 6291464 | tf_op jit(solution)/shard_map/ppermute | solution.py:12
  992.2 90.3 %collective-permute-start.28 = (f32[2,512,512]{2,1,0:T(8,128)S(1)}, f32[2,512,512]{2,1,0:T(8,128)S(1)}, u32[]{:S(2)}, u32[]{:S(2)}) collective-permute-start(f32[2,512,512]{2,1,0:T(8,128)S(1)} %get-tuple-element.9), channel_id=1, source_target_pairs={{0,32},{4,36},{8,40},{12,44},{16,48},{20,52},{24,56},{28,60},{32,0... | collective-permute-start | bytes 6291464 | tf_op jit(solution)/shard_map/ppermute | solution.py:12
  1083.7 46.1 %collective-permute-start.29 = (f32[2,512,512]{2,1,0:T(8,128)S(1)}, f32[2,512,512]{2,1,0:T(8,128)S(1)}, u32[]{:S(2)}, u32[]{:S(2)}) collective-permute-start(f32[2,512,512]{2,1,0:T(8,128)S(1)} %get-tuple-element.8), channel_id=1, source_target_pairs={{0,64},{4,68},{8,72},{12,76},{16,80},{20,84},{24,88},{28,92},{32,9... | collective-permute-start | bytes 6291464 | tf_op jit(solution)/shard_map/ppermute | solution.py:12
  1084.0 90.6 %collective-permute-start.30 = (f32[2,512,512]{2,1,0:T(8,128)S(1)}, f32[2,512,512]{2,1,0:T(8,128)S(1)}, u32[]{:S(2)}, u32[]{:S(2)}) collective-permute-start(f32[2,512,512]{2,1,0:T(8,128)S(1)} %get-tuple-element.7), channel_id=1, source_target_pairs={{0,64},{4,68},{8,72},{12,76},{16,80},{20,84},{24,88},{28,92},{32,9... | collective-permute-start | bytes 6291464 | tf_op jit(solution)/shard_map/ppermute | solution.py:12
  (11 other events, 502.1 us)
Sparse Core Ops, SparseCore 0:
  9.0 51.1 all-gather.1
where the time goes:
time: 1190 us; the launch traced here: 1180 us
  waiting for transfers between devices  914 us (77%)
  matrix products  134 us (11%)
  other arithmetic  73.6 us (6%)
  starting transfers between devices  45 us (4%)
  between operations  14.7 us (1%)
    ppermute x30, waiting for transfers between devices, swapped(): lax.ppermute(array, axis, [(i, i ^ 1 << apart) for i in range(lax.axis_si...  868 us
    all_gather x1, waiting for transfers between devices, local(): lax.all_gather(tokens, 'chan', axis=1, tiled=True)  44.1 us
    ppermute x30, starting transfers between devices, swapped(): lax.ppermute(array, axis, [(i, i ^ 1 << apart) for i in range(lax.axis_si...  41 us
    select_n x5, other arithmetic, pair_forward(): real_part = jnp.where(is_upper, rot_real, real_part + other_real)  30.5 us
    select_n x5, other arithmetic, pair_forward(): imag_part = jnp.where(is_upper, rot_imag, imag_part + other_imag)  29.2 us
    dot_general x2, matrix products, local_forward(): jnp.einsum('rj,ejc->erc', cos_tab, imag_part, precision=precise)  23.9 us
  transfers between devices with their start and end apart: 32, of which 24 were waited for; matrix products, arithmetic and copies ran while one was open for 11% of the time, Pallas kernels for 0%

commit v1 on v0

v1 whole, which is shorter than its diff:
```python
import jax
import jax.numpy as jnp
import numpy as np
from jax import lax
from jax.sharding import PartitionSpec as P

exact = lax.Precision.HIGHEST
SIDE = 128


def transform_tables():
    n = np.arange(SIDE)
    odd = n + 0.5
    first = -2.0 * np.pi / (2 * SIDE) * np.outer(odd, n)
    turn = -2.0 * np.pi / (2 * SIDE * SIDE) * np.outer(odd, n)
    second = -2.0 * np.pi / SIDE * np.outer(n, n)
    wide = np.concatenate([np.cos(first), np.sin(first)], 0)
    cos2, sin2 = np.cos(second), np.sin(second)
    mix = np.block([[cos2, sin2], [-sin2, cos2]])
    back = np.block([[cos2, -sin2], [sin2, cos2]]) / (SIDE * SIDE)
    return [np.asarray(a, np.float32) for a in (wide, np.cos(turn), np.sin(turn), mix, back)]


def forward(x, tables):
    wide, cosine, sine, mix, _ = tables
    a = jnp.einsum("kn,cnm->ckm", wide, x, precision=exact)
    re, im = a[:, :SIDE], a[:, SIDE:]
    turned = jnp.concatenate([re * cosine - im * sine, re * sine + im * cosine], axis=2)
    b = jnp.einsum("ckm,mf->ckf", turned, mix, precision=exact)
    return b[:, :, :SIDE], b[:, :, SIDE:]


def inverse(re, im, tables):
    wide, cosine, sine, _, back = tables
    c = jnp.einsum("ckf,fm->ckm", jnp.concatenate([re, im], axis=2), back, precision=exact)
    re, im = c[:, :, :SIDE], c[:, :, SIDE:]
    turned = jnp.concatenate([re * cosine + im * sine, im * cosine - re * sine], axis=1)
    return jnp.einsum("kn,ckm->cnm", wide, turned, precision=exact)


def local(tokens, in_weight, short_weight, filter_taps, skip_gain):
    rows, channels = filter_taps.shape
    seq_count = lax.axis_size("seq")
    own = channels // seq_count
    tables = transform_tables()

    def to_channels(values):
        parts = values.astype(jnp.bfloat16).T.reshape(seq_count, own, rows)
        parts = lax.all_to_all(parts, "seq", 0, 0, tiled=True)
        return parts.astype(jnp.float32).transpose(1, 0, 2).reshape(own, SIDE, SIDE)

    filter_re, filter_im = forward(to_channels(filter_taps), tables)
    projected = jnp.einsum(
        "td,dgc->tgc",
        lax.all_gather(tokens, "chan", axis=1, tiled=True),
        in_weight,
        preferred_element_type=jnp.float32,
    ).astype(jnp.bfloat16)
    pairs = [(i, i + 1) for i in range(seq_count - 1)]
    previous = lax.ppermute(projected[rows - 2 :], "seq", pairs)
    extended = jnp.concatenate([previous, projected], axis=0).astype(jnp.float32)
    shorted = (
        short_weight[0] * extended[2:]
        + short_weight[1] * extended[1:-1]
        + short_weight[2] * extended[:-2]
    ).astype(jnp.bfloat16)
    short_f32 = shorted.astype(jnp.float32)
    mixed_in = short_f32[:, 1] * short_f32[:, 2]
    data_re, data_im = forward(to_channels(mixed_in), tables)
    prod_re = data_re * filter_re - data_im * filter_im
    prod_im = data_re * filter_im + data_im * filter_re
    result = inverse(prod_re, prod_im, tables)
    parts = result.reshape(own, seq_count, rows).transpose(1, 0, 2).astype(jnp.bfloat16)
    parts = lax.all_to_all(parts, "seq", 0, 0, tiled=True)
    conv_vals = parts.reshape(channels, rows).T.astype(jnp.float32)
    return ((conv_vals + skip_gain * mixed_in) * short_f32[:, 0]).astype(jnp.bfloat16)


def solution(mesh):
    return jax.shard_map(
        local,
        mesh=mesh,
        in_specs=(
            P("seq", "chan"),
            P(None, None, "chan"),
            P(None, None, "chan"),
            P("seq", "chan"),
            P("chan"),
        ),
        out_specs=P("seq", "chan"),
        check_vma=False,
    )
```

time: 1190 us -> 158 us (0.13)
  waiting for transfers between devices: 914 us -> 44.3 us
  matrix products: 134 us -> 28.4 us
  other arithmetic: 73.6 us -> 7.3 us
  starting transfers between devices: 45 us -> 22.1 us
  local copies, waits for them, and re-layouts: 3.5 us -> 23.9 us
  blocking collectives: 0 us -> 17 us
    ppermute x31 -> x1, waiting for transfers between devices: 869 us -> 0.73 us  [local(): previous = lax.ppermute(projected[rows - 2:], 'seq', pairs)]
    dot_general x12 -> x5, matrix products: 123 us -> 14.1 us  [the longest x2 6.98 us: forward(): b = jnp.einsum('ckm,mf->ckf', turned, mix, precision=exact)]
    select_n x15 -> x0, other arithmetic: 65.5 us -> none  [the longest x5 30.5 us: pair_forward(): real_part = jnp.where(is_upper, rot_real, real_part + other_real)]
    ppermute x31 -> x1, starting transfers between devices: 45 us -> 3.91 us  [local(): previous = lax.ppermute(projected[rows - 2:], 'seq', pairs)]
    all_to_all x0 -> x2, starting transfers between devices: none -> 18.2 us  [to_channels(): parts = lax.all_to_all(parts, 'seq', 0, 0, tiled=True)]
    all_to_all x0 -> x1, blocking collectives: none -> 17 us  [local(): parts = lax.all_to_all(parts, 'seq', 0, 0, tiled=True)]
  transfers between devices with their start and end apart: 32 -> 4, of which waited for: 24 -> 3; matrix products, arithmetic and copies ran while one was open for 11% -> 17% of each run, Pallas kernels for 0% -> 0%
where the time goes in v1:
time: 158 us; the launch traced here: 157 us
  waiting for transfers between devices  44.3 us (28%)
  matrix products  28.4 us (18%)
  local copies, waits for them, and re-layouts  23.9 us (15%)
  starting transfers between devices  22.1 us (14%)
  blocking collectives  17 us (11%)
  between operations  13.6 us (9%)
  other arithmetic  7.3 us (5%)
    all_gather x1, waiting for transfers between devices, local(): lax.all_gather(tokens, 'chan', axis=1, tiled=True)  41.1 us
    all_to_all x2, starting transfers between devices, to_channels(): parts = lax.all_to_all(parts, 'seq', 0, 0, tiled=True)  18.2 us
    all_to_all x1, blocking collectives, local(): parts = lax.all_to_all(parts, 'seq', 0, 0, tiled=True)  17 us
    dot_general x1, matrix products, local(): jnp.einsum('td,dgc->tgc', lax.all_gather(tokens, 'chan', axis=1, tiled=Tr...  10.9 us
    dot_general x2, matrix products, forward(): b = jnp.einsum('ckm,mf->ckf', turned, mix, precision=exact)  6.98 us
    reshape x3, local copies, waits for them, and re-layouts, to_channels(): return parts.astype(jnp.float32).transpose(1, 0, 2).reshape(own, SIDE, SIDE)  6.37 us
    convert_element_type x3, local copies, waits for them, and re-layouts, local(): result.reshape(own, seq_count, rows).transpose(1, 0, 2).astype(jnp.bfloat16)  5.52 us
    transpose x2, local copies, waits for them, and re-layouts, to_channels(): return parts.astype(jnp.float32).transpose(1, 0, 2).reshape(own, SIDE, SIDE)  4.25 us
  transfers between devices with their start and end apart: 4, of which 3 were waited for; matrix products, arithmetic and copies ran while one was open for 17% of the time, Pallas kernels for 0%

profile of v1, /device:TPU:1, one launch (start us, length us, event | category | flops | bytes accessed | tf_op | source)
XLA Modules:
  0.0 156.6 jit_solution(4305946872558617440)
XLA Ops:
  6.5 0.7 all-gather.2.cloned.1.call-update
  7.3 2.2 %copy.35 = bf16[512,512]{0,1:T(8,128)(2,1)} copy(f32[512,512]{1,0:T(8,128)} %param.16) | data formatting | bytes 1572864 | tf_op args[3]
  9.5 9.6 %all-to-all-start.1 = ((bf16[32,16,512]{2,1,0:T(8,128)(2,1)}), bf16[32,16,512]{2,1,0:T(8,128)(2,1)}, u32[]{:S(2)}, u32[]{:S(2)}) async-start(bf16[32,16,512]{2,1,0:T(8,128)(2,1)} %bitcast.12), calls=%async_computation.1 | async-start | bytes 1048576 | tf_op jit(solution)/shard_map/all_to_all | solution.py:49
  19.2 41.1 %all-gather.2.cloned.1.call-done = bf16[512,4096]{1,0:T(8,128)(2,1)} async-done(((bf16[512,1024]{1,0:T(8,128)(2,1)}), bf16[512,4096]{1,0:T(8,128)(2,1)}) %all-gather.2.cloned.1.call-update) | async-done | bytes 4194320 | tf_op jit(solution)/shard_map/all_gather | solution.py:55
  60.2 10.9 %fusion.21 = bf16[512,3,512]{2,0,1:T(8,128)(2,1)S(1)} fusion(bf16[4096,3,512]{2,0,1:T(8,128)(2,1)} %param.14, bf16[512,4096]{1,0:T(8,128)(2,1)} %all-gather.2.cloned.1.call-done), kind=kOutput, calls=%fused_computation.24 | convolution fusion | flops 6443237376 | bytes 18350080 | tf_op jit(solution)/shard_map/td,dgc->tgc/dot_general | solution.py:53
  71.1 3.9 %collective-permute-start = (bf16[2,3,512]{2,0,1:T(2,128)(2,1)S(1)}, bf16[2,3,512]{2,0,1:T(2,128)(2,1)S(1)}, u32[]{:S(2)}, u32[]{:S(2)}) collective-permute-start(bf16[2,3,512]{2,0,1:T(2,128)(2,1)S(1)} %slice.80), channel_id=1, source_target_pairs={{0,4},{4,8},{8,12},{12,16},{16,20},{20,24},{24,28},{28,32},{32,36}... | collective-permute-start | bytes 18440 | tf_op jit(solution)/shard_map/ppermute | solution.py:60
  75.1 0.7 collective-permute-done
  76.3 0.9 fusion.24
  77.2 0.9 convert_bitcast_fusion
  78.2 2.0 %copy.31 = bf16[512,512]{1,0:T(8,128)(2,1)} copy(bf16[512,512]{0,1:T(8,128)(2,1)} %convert_bitcast_fusion) | data formatting | bytes 1048576 | tf_op jit(solution)/shard_map/transpose | solution.py:48
  80.2 8.5 %all-to-all-start = ((bf16[32,16,512]{2,1,0:T(8,128)(2,1)}), bf16[32,16,512]{2,1,0:T(8,128)(2,1)}, u32[]{:S(2)}, u32[]{:S(2)}) async-start(bf16[32,16,512]{2,1,0:T(8,128)(2,1)} %bitcast.62), calls=%async_computation | async-start | bytes 1048576 | tf_op jit(solution)/shard_map/all_to_all | solution.py:49
  88.8 2.1 %copy.36 = bf16[16,32,512]{2,1,0:T(8,128)(2,1)} copy(bf16[16,32,512]{2,0,1:T(8,128)(2,1)} %bitcast.13) | data formatting | bytes 1048576 | tf_op jit(solution)/shard_map/transpose | solution.py:50
  90.9 2.1 %reshape.24 = bf16[16,128,128]{2,1,0:T(8,128)(2,1)} reshape(bf16[16,32,512]{2,1,0:T(8,128)(2,1)} %copy.36) | data formatting | bytes 1048576 | tf_op jit(solution)/shard_map/reshape | solution.py:50
  93.0 2.0 %copy.37 = bf16[16,128,128]{1,2,0:T(8,128)(2,1)} copy(bf16[16,128,128]{2,1,0:T(8,128)(2,1)} %reshape.24) | data formatting | bytes 1048576 | tf_op jit(solution)/shard_map/reshape | solution.py:50
  95.1 3.4 %fusion.38 = f32[256,2048]{0,1} fusion(f32[256,128]{1,0:T(8,128)S(1)} %copy-done.6, bf16[128,2048]{0,1:T(8,128)(2,1)} %bitcast.64), kind=kOutput, calls=%fused_computation.53 | convolution fusion | flops 805306368 | bytes 2752512
  98.5 1.7 %all-to-all-done = bf16[32,16,512]{2,1,0:T(8,128)(2,1)} async-done(((bf16[32,16,512]{2,1,0:T(8,128)(2,1)}), bf16[32,16,512]{2,1,0:T(8,128)(2,1)}, u32[]{:S(2)}, u32[]{:S(2)}) %all-to-all-start) | async-done | bytes 524320 | tf_op jit(solution)/shard_map/all_to_all | solution.py:49
  100.2 2.1 %copy.32 = bf16[16,32,512]{2,1,0:T(8,128)(2,1)} copy(bf16[16,32,512]{2,0,1:T(8,128)(2,1)} %bitcast.7) | data formatting | bytes 1048576 | tf_op jit(solution)/shard_map/transpose | solution.py:50
  102.3 2.2 %reshape.22 = bf16[16,128,128]{2,1,0:T(8,128)(2,1)} reshape(bf16[16,32,512]{2,1,0:T(8,128)(2,1)} %copy.32) | data formatting | bytes 1048576 | tf_op jit(solution)/shard_map/reshape | solution.py:50
  104.5 2.2 %convolution_bitcast_fusion = f32[16,256,128]{1,2,0:T(8,128)S(1)} fusion(bf16[16,128,128]{2,1,0:T(8,128)(2,1)} %reshape.22, f32[256,128,1]{1,0,2:T(8,128)S(1)} %copy-done.2), kind=kOutput, calls=%fused_computation.25 | convolution fusion | flops 805306368 | bytes 2752512 | tf_op jit(solution)/shard_map/kn,cnm->ckm/dot_general | solution.py:26
  106.8 0.6 multiply_subtract_fusion.3
  107.8 3.5 %fusion.5 = f32[16,128,256]{2,1,0:T(8,128)S(1)} fusion(f32[256,256,1]{1,0,2:T(8,128)S(1)} %copy-done.1, f32[16,128,128]{1,2,0:T(8,128)S(1)} %get-tuple-element.10, f32[16,128,128]{1,2,0:T(8,128)S(1)} %get-tuple-element.9), kind=kOutput, calls=%fused_computation.8 | convolution fusion | flops 1611137024 | bytes 4456448 | tf_op jit(solution)/shard_map/ckm,mf->ckf/dot_general | solution.py:29
  111.3 3.4 %fusion.9 = f32[16,128,256]{2,1,0:T(8,128)S(1)} fusion(f32[256,256,1]{1,0,2:T(8,128)S(1)} %copy-done.1, f32[16,128,128]{1,2,0:T(8,128)S(1)} %get-tuple-element.13, f32[16,128,128]{1,2,0:T(8,128)S(1)} %get-tuple-element.14), kind=kOutput, calls=%fused_computation.12 | convolution fusion | flops 1611137024 | bytes 4456448 | tf_op jit(solution)/shard_map/ckm,mf->ckf/dot_general | solution.py:29
  115.1 0.6 copy-done.5
  115.7 2.3 %fusion.13 = f32[16,128,256]{1,2,0:T(8,128)S(1)} fusion(f32[256,256,1]{1,0,2:T(8,128)S(1)} %copy-done.5, f32[16,128,128]{2,1,0:T(8,128)S(1)} %get-tuple-element.6, f32[16,128,128]{2,1,0:T(8,128)S(1)} %get-tuple-element.5), kind=kOutput, calls=%fused_computation.16 | convolution fusion | flops 1611137024 | bytes 4456448 | tf_op jit(solution)/shard_map/ckf,fm->ckm/dot_general | solution.py:35
  118.4 2.6 %fusion.28 = bf16[16,128,128]{1,2,0:T(8,128)(2,1)} fusion(f32[256,128,1]{1,0,2:T(8,128)S(1)} %copy-done.2, f32[16,128,128]{1,2,0:T(8,128)S(1)} %get-tuple-element.8, f32[16,128,128]{1,2,0:T(8,128)S(1)} %get-tuple-element.7), kind=kOutput, calls=%fused_computation.29 | convolution fusion | flops 806092800 | bytes 2752512 | tf_op jit(solution)/shard_map/kn,ckm->cnm/dot_general | solution.py:38
  121.0 2.0 %copy.41 = bf16[16,128,128]{2,1,0:T(8,128)(2,1)} copy(bf16[16,128,128]{1,2,0:T(8,128)(2,1)} %fusion.28) | data formatting | bytes 1048576 | tf_op jit(solution)/shard_map/convert_element_type | solution.py:73
  123.0 2.1 %convert_element_type.52 = bf16[16,32,512]{2,1,0:T(8,128)(2,1)} reshape(bf16[16,128,128]{2,1,0:T(8,128)(2,1)} %copy.41) | data formatting | bytes 1048576 | tf_op jit(solution)/shard_map/convert_element_type | solution.py:73
  125.1 1.3 copy.42
  126.5 17.0 %all_to_all.15 = bf16[32,16,512]{2,1,0:T(8,128)(2,1)S(1)} all-to-all(bf16[32,16,512]{2,1,0:T(8,128)(2,1)S(1)} %copy.42), channel_id=1, replica_groups=mesh['seq'=32,'chan'=4] {'seq'}, dimensions={0} | all-to-all | bytes 1048576 | tf_op jit(solution)/shard_map/all_to_all | solution.py:74
  143.5 1.2 bitcast_convert_fusion
  144.7 2.5 %copy.43 = f32[512,512]{0,1:T(8,128)} copy(f32[512,512]{1,0:T(8,128)} %bitcast_convert_fusion) | data formatting | bytes 2097152 | tf_op jit(solution)/shard_map/convert_element_type | solution.py:75
  147.2 2.5 %fusion.32 = bf16[512,512]{1,0:T(8,128)(2,1)} fusion(f32[512,3,512]{2,0,1:T(8,128)S(1)} %fusion.24, f32[512,512]{0,1:T(8,128)} %copy.43, f32[512]{0:T(512)S(1)} %copy-done.8), kind=kLoop, calls=%fused_computation.32 | loop fusion | flops 1310720 | bytes 4720640 | tf_op jit(solution)/shard_map/convert_element_type | solution.py:76
  (24 shorter events, 1.5 us)
Async XLA Ops:
  6.5 53.7 %all-gather.2.cloned.1.call-start = ((), (), s32[]{:S(2)}) async-start(), calls=%async_computation.3 | async-start | bytes 5242880 | tf_op jit(solution)/shard_map/all_gather | solution.py:55
  9.5 70.7 %all-to-all-start.1 = ((bf16[32,16,512]{2,1,0:T(8,128)(2,1)}), bf16[32,16,512]{2,1,0:T(8,128)(2,1)}, u32[]{:S(2)}, u32[]{:S(2)}) async-start(bf16[32,16,512]{2,1,0:T(8,128)(2,1)} %bitcast.12), calls=%async_computation.1 | async-start | bytes 1048576 | tf_op jit(solution)/shard_map/all_to_all | solution.py:49
  19.1 55.9 %copy-start.7 = (f32[3,3,512]{2,1,0:T(4,128)S(1)}, f32[3,3,512]{2,1,0:T(4,128)}, u32[]{:S(2)}) copy-start(f32[3,3,512]{2,1,0:T(4,128)} %param.15) | copy-start | bytes 55300
  71.1 4.7 %collective-permute-start = (bf16[2,3,512]{2,0,1:T(2,128)(2,1)S(1)}, bf16[2,3,512]{2,0,1:T(2,128)(2,1)S(1)}, u32[]{:S(2)}, u32[]{:S(2)}) collective-permute-start(bf16[2,3,512]{2,0,1:T(2,128)(2,1)S(1)} %slice.80), channel_id=1, source_target_pairs={{0,4},{4,8},{8,12},{12,16},{16,20},{20,24},{24,28},{28,32},{32,36}... | collective-permute-start | bytes 18440 | tf_op jit(solution)/shard_map/ppermute | solution.py:60
  80.2 14.9 %copy-start.6 = (f32[256,128]{1,0:T(8,128)S(1)}, f32[256,128]{1,0:T(8,128)}, u32[]{:S(2)}) copy-start(f32[256,128]{1,0:T(8,128)} %constant.10.clone) | copy-start | bytes 393220
  80.2 20.0 %all-to-all-start = ((bf16[32,16,512]{2,1,0:T(8,128)(2,1)}), bf16[32,16,512]{2,1,0:T(8,128)(2,1)}, u32[]{:S(2)}, u32[]{:S(2)}) async-start(bf16[32,16,512]{2,1,0:T(8,128)(2,1)} %bitcast.62), calls=%async_computation | async-start | bytes 1048576 | tf_op jit(solution)/shard_map/all_to_all | solution.py:49
  95.1 9.5 %copy-start.2 = (f32[256,128,1]{1,0,2:T(8,128)S(1)}, f32[256,128,1]{1,0,2:T(8,128)}, u32[]{:S(2)}) copy-start(f32[256,128,1]{1,0,2:T(8,128)} %constant.15) | copy-start | bytes 393220
  102.3 4.4 %copy-start.3 = (f32[128,128]{0,1:T(8,128)S(1)}, f32[128,128]{0,1:T(8,128)}, u32[]{:S(2)}) copy-start(f32[128,128]{0,1:T(8,128)} %constant.12.clone) | copy-start | bytes 196612
  102.3 4.4 %copy-start.4 = (f32[128,128]{0,1:T(8,128)S(1)}, f32[128,128]{0,1:T(8,128)}, u32[]{:S(2)}) copy-start(f32[128,128]{0,1:T(8,128)} %constant.11.clone) | copy-start | bytes 196612
  104.5 2.3 %copy-start = (f32[256,2048]{0,1:S(1)}, f32[256,2048]{0,1}, u32[]{:S(2)}) copy-start(f32[256,2048]{0,1} %fusion.38) | copy-start | bytes 6291460
  106.8 1.0 copy-start.1
  114.8 1.0 copy-start.5
  143.5 3.7 %copy-start.8 = (f32[512]{0:T(512)S(1)}, f32[512]{0:T(512)}, u32[]{:S(2)}) copy-start(f32[512]{0:T(512)} %param.17) | copy-start | bytes 6148
Sparse Core Ops, SparseCore 0:
  9.0 51.1 all-gather.1
